TPU v7x, 128 devices: a whole 4x4x4 slice. The times are simulated.
128 devices in a mesh: row: 8 (over z, core), col: 16 (over y, x).
Axes of the slice: x: 4, y: 4, z: 4, core: 2. Of those that a mesh axis runs over, the one named last changes fastest.
Arguments:
- singles: bfloat16 [1024, 384], P('row', 'col'), may hold values from -6 to 6
- pair_in: bfloat16 [1024, 1024, 128], P('row', 'col'), may hold values from -6 to 6
- proj_weight: bfloat16 [384, 256], P('col'), may hold values from -0.3125 to 0.3125
- gain_first: float32 [128], replicated, may hold values from 0.1 to 1.9
- first_in: bfloat16 [128, 1024], replicated, may hold values from -0.5 to 0.5
- first_out: bfloat16 [512, 128], replicated, may hold values from -0.25 to 0.25
- gain_second: float32 [128], replicated, may hold values from 0.1 to 1.9
- second_in: bfloat16 [128, 1024], replicated, may hold values from -0.5 to 0.5
- second_out: bfloat16 [512, 128], replicated, may hold values from -0.25 to 0.25
- head_weight: bfloat16 [128, 64], replicated, may hold values from -1.5 to 1.5
- pae_bins: int32 [1024, 1024], P('row', 'col'), may hold values from 0 to 63
- chain_perm: int32 [1024], replicated, may hold values from 0 to 1023, as said below
- resolved_counts: int32 [8, 16], P('row'), may hold values from 1 to 256, 2048 in all within a row
- tile_order: int32 [8, 4096], P('row', 'col'), may hold values from 0 to 255, as said below
Outputs:
- pair_grad: bfloat16 [1024, 1024, 128], P('row', 'col')
- single_grad: float32 [1024, 384], P('row', 'col')
- second_in_grad: float32 [128, 1024], replicated
- second_out_grad: float32 [512, 128], replicated
- head_grad: float32 [128, 64], replicated
Inputs may be any that keep to these rules, and one draw needn't show every extreme that they name: chain_perm maps every aligned group of 64 tokens onto itself, moving whole aligned runs of 16 tokens and keeping the order inside a run. Each row of resolved_counts sums to 2048, and its largest entry is 256. In each row of tile_order, entries b * 256 to (b + 1) * 256 - 1 are a permutation of 0 to 255.
All inputs are finite; a program needn't handle non-finite values.
Results may differ from a plain program's by a relative error of at most 0.011.
Values may be sent and summed in bfloat16 or wider, within the bound.
A program may use at most 64 MiB of HBM per device.

v0:
```python
import jax
import jax.numpy as jnp
from jax import lax
from jax.sharding import PartitionSpec as P

TILE = 32


def contract(left_op, right_op, left_dim, right_dim):
    return lax.dot_general(
        left_op,
        right_op,
        (((left_dim,), (right_dim,)), ((), ())),
        preferred_element_type=jnp.float32,
    )


def block_size(extent, per_item, limit):
    best = 1
    for candidate in range(1, extent + 1):
        if extent % candidate == 0 and candidate * per_item <= limit:
            best = candidate
    return best


def transition_forward(start_z, gain_vec, w_in, w_out):
    hidden_units = w_out.shape[0]
    average = jnp.mean(start_z, axis=-1, keepdims=True)
    centred = start_z - average
    scaling = lax.rsqrt(jnp.mean(centred * centred, axis=-1, keepdims=True) + 1e-05)
    normed = centred * scaling
    inputs = (normed * gain_vec).astype(jnp.bfloat16)
    gate_up = jnp.dot(inputs, w_in, preferred_element_type=jnp.float32)
    gate_part = gate_up[:, :hidden_units]
    up_part = gate_up[:, hidden_units:]
    gate_sig = jax.nn.sigmoid(gate_part)
    hidden_act = (gate_part * gate_sig * up_part).astype(jnp.bfloat16)
    result = jnp.dot(hidden_act, w_out, preferred_element_type=jnp.float32)
    return (result, (normed, scaling, inputs, gate_part, up_part, gate_sig, hidden_act))


def transition_backward(saved, grad_out, gain_vec, w_in, w_out, with_weights):
    normed, scaling, inputs, gate_part, up_part, gate_sig, hidden_act = saved
    grad_hidden = contract(grad_out, w_out, 1, 1)
    grad_gate = grad_hidden * up_part * gate_sig * (1.0 + gate_part * (1.0 - gate_sig))
    grad_up = grad_hidden * gate_part * gate_sig
    grad_both = jnp.concatenate([grad_gate, grad_up], axis=1).astype(jnp.bfloat16)
    grad_normed = contract(grad_both, w_in, 1, 1) * gain_vec
    grad_field = scaling * (
        grad_normed
        - jnp.mean(grad_normed, axis=-1, keepdims=True)
        - normed * jnp.mean(grad_normed * normed, axis=-1, keepdims=True)
    )
    if with_weights:
        return (grad_field, contract(inputs, grad_both, 0, 0), contract(hidden_act, grad_out, 0, 0))
    return (grad_field, None, None)


def head_step(rounded_z, targets, keep_mask, head_weight):
    logits = jnp.dot(rounded_z, head_weight, preferred_element_type=jnp.float32)
    exponent = jnp.exp(logits - jnp.max(logits, axis=-1, keepdims=True))
    probability = exponent / jnp.sum(exponent, axis=-1, keepdims=True)
    onehot = (targets[:, None] == lax.broadcasted_iota(jnp.int32, logits.shape, 1)).astype(
        jnp.float32
    )
    grad_logits = ((probability - onehot) * keep_mask[:, None]).astype(jnp.bfloat16)
    return (
        contract(grad_logits, head_weight, 1, 1).astype(jnp.bfloat16),
        contract(rounded_z, grad_logits, 0, 0),
    )


def second_step(pair_one, targets, live_mask, gain_second, second_in, second_out, head_weight):
    start_f = pair_one.astype(jnp.float32)
    delta, saved = transition_forward(start_f, gain_second, second_in, second_out)
    rounded_z = (start_f + live_mask[:, None] * delta).astype(jnp.bfloat16)
    grad_two, head_part = head_step(rounded_z, targets, jnp.ones_like(live_mask), head_weight)
    masked_out = jnp.where(live_mask[:, None] > 0, grad_two, jnp.zeros((), jnp.bfloat16))
    back_field, in_part, out_part = transition_backward(
        saved, masked_out, gain_second, second_in, second_out, True
    )
    return (
        (grad_two.astype(jnp.float32) + back_field).astype(jnp.bfloat16),
        in_part,
        out_part,
        head_part,
    )


def local(
    singles,
    pair_in,
    proj_weight,
    gain_first,
    first_in,
    first_out,
    gain_second,
    second_in,
    second_out,
    head_weight,
    pae_bins,
    chain_perm,
    resolved_counts,
    tile_order,
):
    rows_dev, cols_dev, width = pair_in.shape
    tile_len = TILE
    tiles_dev = rows_dev * cols_dev // tile_len
    token_count = chain_perm.shape[0]
    row_index = lax.axis_index("row")
    col_index = lax.axis_index("col")
    col_count = lax.axis_size("col")
    partial_proj = jnp.dot(singles, proj_weight, preferred_element_type=jnp.float32)
    projected = lax.psum(partial_proj, "col")
    left_part = projected[:, :width]
    right_part = projected[:, width:].astype(jnp.bfloat16)
    col_start = col_index * cols_dev
    right_all = lax.all_gather(right_part, "row", axis=0, tiled=True)
    col_right = lax.dynamic_slice_in_dim(right_all, col_start, cols_dev, 0)
    col_right_f = col_right.astype(jnp.float32)
    block_rows = block_size(rows_dev, cols_dev, 1024)
    row_blocks = rows_dev // block_rows
    block_pairs = block_rows * cols_dev

    def start_field(block_index):
        first_row = block_index * block_rows
        pair_rows = lax.dynamic_slice_in_dim(pair_in, first_row, block_rows, 0).astype(jnp.float32)
        left_rows = lax.dynamic_slice_in_dim(left_part, first_row, block_rows, 0)
        field_rows = pair_rows + left_rows[:, None, :] + col_right_f[None, :, :]
        return field_rows.reshape(block_pairs, width)

    def forward_block(block_index):
        start_z = start_field(block_index)
        delta, unused_saved = transition_forward(start_z, gain_first, first_in, first_out)
        return (start_z + delta).astype(jnp.bfloat16)

    block_ids = jnp.arange(row_blocks, dtype=jnp.int32)
    pair_one = lax.map(forward_block, block_ids).reshape(rows_dev * cols_dev, width)
    live_count = resolved_counts[0, col_index]
    order_list = tile_order[0]
    tile_iota = jnp.arange(tiles_dev, dtype=jnp.int32)
    rank_of = jnp.sum(
        jnp.where(order_list[None, :] == tile_iota[:, None], tile_iota[None, :], 0), axis=1
    )
    tile_live = rank_of < live_count
    pair_live = jnp.repeat(tile_live, tile_len).astype(jnp.float32)
    perm_rows = (
        lax.dynamic_slice_in_dim(chain_perm, row_index * rows_dev, rows_dev, 0)
        - row_index * rows_dev
    )
    perm_cols = lax.dynamic_slice_in_dim(chain_perm, col_start, cols_dev, 0) - col_start
    targets = jnp.take(jnp.take(pae_bins, perm_rows, axis=0), perm_cols, axis=1).reshape(
        rows_dev * cols_dev
    )
    pair_stack = pair_one.reshape(row_blocks, block_pairs, width)
    target_stack = targets.reshape(row_blocks, block_pairs)
    live_stack = pair_live.reshape(row_blocks, block_pairs)
    zero_in = jnp.zeros(second_in.shape, jnp.float32)
    zero_out = jnp.zeros(second_out.shape, jnp.float32)
    zero_head = jnp.zeros(head_weight.shape, jnp.float32)

    def head_block(running, operands):
        grad_two, head_part = head_step(operands[0], operands[1], 1.0 - operands[2], head_weight)
        return (running + head_part, grad_two)

    head_sum, rest_stack = lax.scan(head_block, zero_head, (pair_stack, target_stack, live_stack))
    rest_tiles = rest_stack.reshape(tiles_dev, tile_len, width)
    slots = -(-tiles_dev // col_count)
    row_counts = resolved_counts[0]
    offsets = jnp.cumsum(row_counts) - row_counts
    my_offset = offsets[col_index]
    worker_iota = jnp.arange(col_count, dtype=jnp.int32)[:, None]
    slot_iota = jnp.arange(slots, dtype=jnp.int32)[None, :]
    send_rank = col_count * slot_iota + jnp.mod(worker_iota - my_offset, col_count)
    send_valid = send_rank < live_count
    send_ids = order_list[jnp.minimum(send_rank, tiles_dev - 1)]
    tile_view = pair_one.reshape(tiles_dev, tile_len, width)
    target_view = targets.reshape(tiles_dev, tile_len).astype(jnp.bfloat16)
    send_pairs = jnp.where(
        send_valid[:, :, None, None], tile_view[send_ids], jnp.zeros((), jnp.bfloat16)
    )
    send_targets = jnp.where(
        send_valid[:, :, None], target_view[send_ids], jnp.zeros((), jnp.bfloat16)
    )
    recv_pairs, recv_targets = (
        lax.all_to_all(send_pairs, "col", split_axis=0, concat_axis=0, tiled=True),
        lax.all_to_all(send_targets, "col", split_axis=0, concat_axis=0, tiled=True),
    )
    work_count = tiles_dev // 2
    position = jnp.arange(work_count, dtype=jnp.int32)
    global_rank = col_count * position + col_index
    source = jnp.sum((offsets[None, :] <= global_rank[:, None]).astype(jnp.int32), axis=1) - 1
    source_slot = (global_rank - offsets[source]) // col_count
    flat_index = source * slots + source_slot
    work_pairs = recv_pairs.reshape(col_count * slots, tile_len, width)[flat_index]
    work_targets = recv_targets.reshape(col_count * slots, tile_len)[flat_index].astype(jnp.int32)
    block_tiles = block_size(work_count, tile_len, 1024)
    work_blocks = work_count // block_tiles
    work_pair_stack = work_pairs.reshape(work_blocks, block_tiles * tile_len, width)
    work_target_stack = work_targets.reshape(work_blocks, block_tiles * tile_len)

    def worker_block(running, operands):
        all_live = jnp.ones(operands[1].shape, jnp.float32)
        grad_one, in_part, out_part, head_part = second_step(
            operands[0], operands[1], all_live, gain_second, second_in, second_out, head_weight
        )
        return ((running[0] + in_part, running[1] + out_part, running[2] + head_part), grad_one)

    weight_sums, work_grad_stack = lax.scan(
        worker_block, (zero_in, zero_out, head_sum), (work_pair_stack, work_target_stack)
    )
    work_grads = work_grad_stack.reshape(work_count, tile_len, width)
    back_rank = col_count * slot_iota + jnp.mod(col_index - offsets[:, None], col_count)
    back_valid = back_rank < row_counts[:, None]
    back_position = jnp.minimum((offsets[:, None] + back_rank) // col_count, work_count - 1)
    back_pairs = jnp.where(
        back_valid[:, :, None, None], work_grads[back_position], jnp.zeros((), jnp.bfloat16)
    )
    returned = lax.all_to_all(back_pairs, "col", split_axis=0, concat_axis=0, tiled=True)
    tile_worker = jnp.mod(my_offset + rank_of, col_count)
    tile_slot = jnp.minimum(rank_of // col_count, slots - 1)
    from_worker = returned.reshape(col_count * slots, tile_len, width)[
        tile_worker * slots + tile_slot
    ]
    grad_one_all = jnp.where(tile_live[:, None, None], from_worker, rest_tiles).reshape(
        rows_dev * cols_dev, width
    )
    grad_one_stack = grad_one_all.reshape(row_blocks, block_pairs, width)

    def backward_block(running, operands):
        block_index, grad_one = operands
        start_z = start_field(block_index)
        unused_delta, saved = transition_forward(start_z, gain_first, first_in, first_out)
        back_field, unused_in, unused_out = transition_backward(
            saved, grad_one, gain_first, first_in, first_out, False
        )
        grad_zero = (grad_one.astype(jnp.float32) + back_field).reshape(block_rows, cols_dev, width)
        return (
            running + jnp.sum(grad_zero, axis=0),
            (grad_zero.astype(jnp.bfloat16), jnp.sum(grad_zero, axis=1)),
        )

    right_grad, (pair_grad_stack, left_stack) = lax.scan(
        backward_block, jnp.zeros((cols_dev, width), jnp.float32), (block_ids, grad_one_stack)
    )
    pair_grad = pair_grad_stack.reshape(rows_dev, cols_dev, width)
    left_grad = left_stack.reshape(rows_dev, width)
    token_part = jnp.zeros((token_count, 2 * width), jnp.float32)
    token_part = lax.dynamic_update_slice(token_part, left_grad, (row_index * rows_dev, 0))
    token_part = lax.dynamic_update_slice(token_part, right_grad, (col_start, width))
    token_total, in_total, out_total, head_total = lax.psum(
        (token_part, weight_sums[0], weight_sums[1], weight_sums[2]), ("row", "col")
    )
    token_rows = lax.dynamic_slice_in_dim(token_total, row_index * rows_dev, rows_dev, 0).astype(
        jnp.bfloat16
    )
    single_grad = contract(token_rows, proj_weight, 1, 1)
    return (
        pair_grad,
        single_grad,
        in_total / token_count,
        out_total / token_count,
        head_total / token_count,
    )


def solution(mesh):
    in_specs = (
        P("row", "col"),
        P("row", "col", None),
        P("col", None),
        P(),
        P(),
        P(),
        P(),
        P(),
        P(),
        P(),
        P("row", "col"),
        P(),
        P("row", None),
        P("row", "col"),
    )
    out_specs = (P("row", "col", None), P("row", "col"), P(), P(), P())
    return jax.shard_map(local, mesh=mesh, in_specs=in_specs, out_specs=out_specs, check_vma=False)
```

profile of v0, /device:TPU:1, one launch (start us, length us, event | category | flops | bytes accessed | tf_op | source)
XLA Modules:
  0.0 618.8 jit_solution(7770418198475508663)
XLA Ops:
  7.9 1.5 fusion.87
  13.8 1.9 gather_fusion.2
  21.9 7.6 %all-to-all-start.1 = ((bf16[16,2,256]{2,1,0:T(2,128)(2,1)}), bf16[16,2,256]{2,1,0:T(2,128)(2,1)S(1)}, u32[]{:S(2)}, u32[]{:S(2)}) async-start(bf16[16,2,256]{2,1,0:T(2,128)(2,1)} %reshape.938), calls=%async_computation.1 | async-start | bytes 32768 | tf_op jit(solution)/shard_map/all_to_all | solution.py:187
  30.6 10.0 %fusion.77 = s32[128]{0:T(128)S(1)} fusion(s32[128]{0:T(128)S(1)} %convert_reduce_fusion.1, s32[]{:T(128)} %bitcast.33, s32[]{:T(128)} %bitcast.34, s32[]{:T(128)} %bitcast.35, s32[]{:T(128)} %bitcast.36, s32[]{:T(128)} %bitcast.37, s32[]{:T(128)} %bitcast.39, s32[]{:T(128)} %bitcast.38, s32[]{:T(128)} %bitcast.16, s32[]{:T(128)} %bitcast.18, s32[]{:T(128)} %bitcast.20, ...), kind=kLoop, calls=%fused_computation.208 | loop fusion | flops 7296 | bytes 1092 | tf_op jit(solution)/shard_map/select_n | solution.py:195
  42.0 54.0 %all-reduce.6.cloned.1.call-done = f32[128,256]{1,0:T(8,128)} async-done(((f32[128,256]{1,0:T(8,128)}), f32[128,256]{1,0:T(8,128)}) %all-reduce.6.cloned.1.call-update) | async-done | bytes 131088 | tf_op jit(solution)/shard_map/psum | solution.py:114
  96.8 15.6 %all_gather.3 = bf16[1024,128]{1,0:T(8,128)(2,1)S(1)} all-gather(bf16[128,128]{1,0:T(8,128)(2,1)S(1)} %slice.95), channel_id=1, replica_groups=mesh['row'=8,'col'=16] {'row'}, dimensions={0}, use_global_device_ids=true | all-gather | bytes 294912 | tf_op jit(solution)/shard_map/all_gather | solution.py:118
  112.5 1.5 slice.72
  113.9 1.6 broadcast.784.clone
  115.5 64.0 %while.55 = (s32[]{:T(128)}, bf16[8,1024,128]{2,1,0:T(8,128)(2,1)}, s32[8]{0:T(128)S(1)}, bf16[128,64,128]{2,1,0:T(8,128)(2,1)}, f32[128,128]{1,0:T(8,128)}, /*i...) while((s32[]{:T(128)}, bf16[8,1024,128]{2,1,0:T(8,128)(2,1)}, ...), condition=%wide.region_6.7_spmd, body=%wide.region_3.6_spmd.sunk | while | flops 407897088 | bytes 11818179 | solution.py:138
  118.7 1.4 multiply_reduce_fusion.5
  121.2 2.3 fusion.163
  126.7 1.4 multiply_reduce_fusion.5
  129.2 2.3 fusion.163
  134.7 1.4 multiply_reduce_fusion.5
  137.2 2.3 fusion.163
  142.7 1.4 multiply_reduce_fusion.5
  145.2 2.3 fusion.163
  153.2 2.3 fusion.163
  158.7 1.4 multiply_reduce_fusion.5
  161.2 2.3 fusion.163
  166.7 1.4 multiply_reduce_fusion.5
  169.2 2.3 fusion.163
  177.2 2.3 fusion.163
  179.6 2.6 gather_fusion.3
  182.2 1.6 broadcast_select_fusion
  183.7 4.8 all-to-all-start
  189.2 22.2 %while.56 = (s32[]{:T(128)}, f32[128,64]{0,1:T(8,128)S(1)}, bf16[8,1024,128]{2,1,0:T(8,128)(2,1)S(1)}, bf16[8,1024,128]{2,1,0:T(8,128)(2,1)}, bf16[128,64]{0,1:T...) while((s32[]{:T(128)}, f32[128,64]{0,1:T(8,128)S(1)}, ...), condition=%wide.region_10.11_spmd.clone, body=%wide.region_7.10_spmd.clone.sunk | while | flops 51592192 | bytes 1995891 | solution.py:166
  211.5 9.9 %all-to-all-done = bf16[16,16,32,128]{3,2,1,0:T(8,128)(2,1)} async-done(((bf16[16,16,32,128]{3,2,1,0:T(8,128)(2,1)}), bf16[16,16,32,128]{3,2,1,0:T(8,128)(2,1)}, u32[]{:S(2)}, u32[]{:S(2)}) %all-to-all-start) | async-done | bytes 2097184 | tf_op jit(solution)/shard_map/all_to_all | solution.py:186
  221.4 2.4 gather_fusion.4
  223.8 45.5 %while.57 = (s32[]{:T(128)}, f32[128,1024]{1,0:T(8,128)}, f32[512,128]{1,0:T(8,128)S(1)}, f32[128,64]{0,1:T(8,128)S(1)}, bf16[4,1024,128]{2,1,0:T(8,128)(2,1)}, ...) while((s32[]{:T(128)}, f32[128,1024]{1,0:T(8,128)}, ...), condition=%wide.region_19.20_spmd.clone, body=%wide.region_12.19_spmd.clone.sunk | while | flops 1282874368 | bytes 39037144 | solution.py:209
  231.5 3.5 fusion.189
  242.8 3.7 fusion.189
  254.2 3.7 fusion.189
  265.6 3.7 fusion.189
  269.3 2.3 gather_fusion.7
  271.6 1.5 broadcast_select_fusion.1
  273.2 3.7 all-to-all-start.2
  278.3 161.1 %all-reduce.8.cloned.1.call-done = (f32[128,1024]{1,0:T(8,128)}, f32[512,128]{1,0:T(8,128)}) async-done(((f32[128,1024]{1,0:T(8,128)}, f32[512,128]{1,0:T(8,128)}), (f32[128,1024]{1,0:T(8,128)}, f32[512,128]{1,0:T(8,128)})) %all-reduce.8.cloned.1.call-update) | async-done | bytes 786448 | tf_op jit(solution)/shard_map/psum | solution.py:251
  439.5 1.7 broadcast_multiply_fusion.8
  441.1 1.9 broadcast_multiply_fusion.7
  443.0 2.2 gather_fusion.8
  445.2 3.6 bitcast_select_fusion
  448.7 89.8 %while.58 = (s32[]{:T(128)}, f32[64,128]{1,0:T(8,128)S(1)}, bf16[8,16,64,128]{3,2,1,0:T(8,128)(2,1)}, f32[8,16,128]{2,1,0:T(8,128)}, bf16[8,1024,128]{2,1,0:T(8,...) while((s32[]{:T(128)}, f32[64,128]{1,0:T(8,128)S(1)}, ...), condition=%wide.region_27.28_spmd.clone, body=%wide.region_20.27_spmd.clone.sunk | while | flops 686169088 | bytes 20674808 | solution.py:243
  451.9 1.4 multiply_reduce_fusion.6
  454.5 2.0 fusion.198
  456.5 1.4 fusion.199
  465.7 2.0 fusion.198
  467.8 1.4 fusion.199
  476.9 2.0 fusion.198
  479.0 1.4 fusion.199
  485.5 1.4 multiply_reduce_fusion.6
  488.2 2.0 fusion.198
  490.2 1.4 fusion.199
  499.4 2.0 fusion.198
  501.4 1.4 fusion.199
  508.0 1.4 multiply_reduce_fusion.6
  510.6 2.0 fusion.198
  512.7 1.4 fusion.199
  521.8 2.0 fusion.198
  523.9 1.4 fusion.199
  530.4 1.4 multiply_reduce_fusion.6
  533.0 2.0 fusion.198
  535.1 1.4 fusion.199
  539.5 71.1 %all-reduce.9 = (bf16[1024,256]{1,0:T(8,128)(2,1)S(1)}, f32[128,64]{0,1:T(8,128)S(1)}) all-reduce(f32[1024,256]{1,0:T(8,128)S(1)} %constant_dynamic-update-slice_fusion.2, f32[128,64]{0,1:T(8,128)S(1)} %get-tuple-element.223), channel_id=1, replica_groups=mesh['row'=8,'col'=16] {'row','col'}, use_global_device_ids=true, to_apply=%region_28.29 | all-reduce | flops 270336 | bytes 1638400 | tf_op jit(solution)/shard_map/psum | solution.py:251
  (440 shorter events, 153.7 us)
Async XLA Ops:
  7.2 0.7 copy-start
  7.2 6.6 %copy-start.1 = (s32[1,256]{1,0:T(1,128)S(1)}, s32[1,256]{1,0:T(1,128)}, u32[]{:S(2)}) copy-start(s32[1,256]{1,0:T(1,128)} %param.35) | copy-start | bytes 3076
  7.2 88.8 %all-reduce.6.cloned.1.call-start = ((), (), s32[]{:S(2)}) async-start(), calls=%async_computation.3 | async-start | bytes 262144 | tf_op jit(solution)/shard_map/psum | solution.py:114
  13.8 3.7 copy-start.9
  13.8 5.6 copy-start.11
  20.2 95.3 %copy-start.2 = (bf16[128,1024]{1,0:T(8,128)(2,1)S(1)}, bf16[128,1024]{1,0:T(8,128)(2,1)}, u32[]{:S(2)}) copy-start(bf16[128,1024]{1,0:T(8,128)(2,1)} %param.26) | copy-start | bytes 786436
  20.2 95.3 %copy-start.8 = (f32[128]{0:T(128)S(1)}, f32[128]{0:T(128)}, u32[]{:S(2)}) copy-start(f32[128]{0:T(128)} %param.25) | copy-start | bytes 1540
  21.9 19.1 %all-to-all-start.1 = ((bf16[16,2,256]{2,1,0:T(2,128)(2,1)}), bf16[16,2,256]{2,1,0:T(2,128)(2,1)S(1)}, u32[]{:S(2)}, u32[]{:S(2)}) async-start(bf16[16,2,256]{2,1,0:T(2,128)(2,1)} %reshape.938), calls=%async_computation.1 | async-start | bytes 32768 | tf_op jit(solution)/shard_map/all_to_all | solution.py:187
  183.7 37.7 %all-to-all-start = ((bf16[16,16,32,128]{3,2,1,0:T(8,128)(2,1)}), bf16[16,16,32,128]{3,2,1,0:T(8,128)(2,1)}, u32[]{:S(2)}, u32[]{:S(2)}) async-start(bf16[16,16,32,128]{3,2,1,0:T(8,128)(2,1)} %broadcast_select_fusion), calls=%async_computation | async-start | bytes 4194304 | tf_op jit(solution)/shard_map/all_to_all | solution.py:186
  188.5 0.7 copy-start.7
  211.4 10.0 %copy-start.4 = (bf16[8,1024,128]{2,1,0:T(8,128)(2,1)}, bf16[8,1024,128]{2,1,0:T(8,128)(2,1)S(1)}, u32[]{:S(2)}) copy-start(bf16[8,1024,128]{2,1,0:T(8,128)(2,1)S(1)} %get-tuple-element.217) | copy-start | bytes 6291460
  211.4 12.3 %copy-start.5 = (bf16[128,1024]{1,0:T(8,128)(2,1)S(1)}, bf16[128,1024]{1,0:T(8,128)(2,1)}, u32[]{:S(2)}) copy-start(bf16[128,1024]{1,0:T(8,128)(2,1)} %param.29) | copy-start | bytes 786436
  211.4 12.3 %copy-start.6 = (bf16[512,128]{1,0:T(8,128)(2,1)S(1)}, bf16[512,128]{1,0:T(8,128)(2,1)}, u32[]{:S(2)}) copy-start(bf16[512,128]{1,0:T(8,128)(2,1)} %param.30) | copy-start | bytes 393220
  211.4 12.3 %copy-start.10 = (f32[128]{0:T(128)S(1)}, f32[128]{0:T(128)}, u32[]{:S(2)}) copy-start(f32[128]{0:T(128)} %param.28) | copy-start | bytes 1540
  228.1 1.4 copy-start.12
  228.1 1.4 copy-start.13
  239.4 1.4 copy-start.12
  239.4 1.4 copy-start.13
  250.8 1.4 copy-start.12
  250.8 1.4 copy-start.13
  262.2 1.4 copy-start.12
  262.2 1.4 copy-start.13
  269.3 2.3 copy-start.3
  273.2 169.8 %all-to-all-start.2 = ((bf16[16,16,32,128]{3,2,1,0:T(8,128)(2,1)}), bf16[16,16,32,128]{3,2,1,0:T(8,128)(2,1)S(1)}, u32[]{:S(2)}, u32[]{:S(2)}) async-start(bf16[16,16,32,128]{3,2,1,0:T(8,128)(2,1)} %broadcast_select_fusion.1), calls=%async_computation.2 | async-start | bytes 4194304 | tf_op jit(solution)/shard_map/all_to_all | solution.py:219
  276.9 162.6 %all-reduce.8.cloned.1.call-start = ((), (), s32[]{:S(2)}) async-start(), calls=%async_computation.4 | async-start | bytes 1572864 | tf_op jit(solution)/shard_map/psum | solution.py:251
Sparse Core Ops, SparseCore 0:
  11.8 84.1 all-reduce.5
  283.0 156.3 all-reduce.7
where the time goes:
time: 623 us; the launch traced here: 619 us
  waiting for transfers between devices  226 us (36%)
  matrix products  115 us (18%)
  other arithmetic  88.6 us (14%)
  blocking collectives  86.7 us (14%)
  local copies, waits for them, and re-layouts  58.9 us (9%)
  starting transfers between devices  16.4 us (3%)
  between operations  14.5 us (2%)
  loops' own time  12.6 us (2%)
    psum x1, waiting for transfers between devices, local(): lax.psum((token_part, weight_sums[0], weight_sums[1], weight_sums[2]), ('...  161 us
    psum x1, blocking collectives, local(): lax.psum((token_part, weight_sums[0], weight_sums[1], weight_sums[2]), ('...  71.1 us
    dot_general x57, matrix products, contract(): lax.dot_general(left_op, right_op, (((left_dim,), (right_dim,)), ((), ())...  68 us
    psum x1, waiting for transfers between devices, local(): projected = lax.psum(partial_proj, 'col')  54 us
    reduce_sum x20, other arithmetic, transition_forward(): jnp.mean(centred * centred, axis=-1, keepdims=True) + 1e-05  23.1 us
    dot_general x12, matrix products, transition_forward(): result = jnp.dot(hidden_act, w_out, preferred_element_type=jnp.float32)  20.6 us
    reduce_sum x20, other arithmetic, transition_forward(): average = jnp.mean(start_z, axis=-1, keepdims=True)  19.2 us
    all_gather x1, blocking collectives, local(): right_all = lax.all_gather(right_part, 'row', axis=0, tiled=True)  15.6 us
  transfers between devices with their start and end apart: 5, of which 3 were waited for; matrix products, arithmetic and copies ran while one was open for 8% of the time, Pallas kernels for 0%

commit v1 on v0

v1 whole, which is shorter than its diff:
```python
import functools
import jax
import jax.numpy as jnp
from jax import lax
from jax.experimental import pallas as pl
from jax.experimental.pallas import tpu as pltpu
from jax.sharding import PartitionSpec as P

TILE = 32
BLOCK_PAIRS = 512
CHUNK = 256
MESH = pl.DeviceIdType.MESH
BF = jnp.bfloat16
F32 = jnp.float32
VM = pl.BlockSpec(memory_space=pltpu.VMEM)
SM = pl.BlockSpec(memory_space=pltpu.SMEM)


def dot(left, right):
    return jnp.dot(left, right, preferred_element_type=F32)


def dot_rows(left, right):
    return lax.dot_general(left, right, (((0,), (0,)), ((), ())), preferred_element_type=F32)


def dot_lanes(left, right):
    return lax.dot_general(left, right, (((1,), (1,)), ((), ())), preferred_element_type=F32)


def prologue(
    n_row,
    n_col,
    singles,
    proj,
    bins,
    perm,
    counts,
    order,
    left_out,
    right_out,
    target_out,
    live_out,
    s_buf,
    w_buf,
    r_buf,
    s_send,
    s_recv,
    w_send,
    w_recv,
    r_send,
    r_recv,
    own_sem,
):
    row, col = lax.axis_index("row"), lax.axis_index("col")
    rows_dev = singles.shape[0]
    half = rows_dev // 2
    source_row = col // 2
    own_half = lax.rem(col, 2)
    own_right = source_row == row
    barrier = pltpu.get_barrier_semaphore()
    for k in range(1, n_col):
        peer = lax.rem(col + k, n_col)
        pl.semaphore_signal(barrier, inc=1, device_id=(row, peer), device_id_type=MESH)
        pl.semaphore_signal(barrier, inc=1, device_id=(source_row, peer), device_id_type=MESH)

    @pl.when(jnp.logical_not(own_right))
    def _():
        pl.semaphore_signal(barrier, inc=1, device_id=(source_row, col), device_id_type=MESH)

    pl.semaphore_wait(barrier, n_col - 1 + 2 * n_row - jnp.where(own_right, 1, 0))

    def s_copy(k):
        return pltpu.make_async_remote_copy(
            singles, s_buf.at[k], s_send.at[k], s_recv.at[k],
            device_id=(row, lax.rem(col + k, n_col)), device_id_type=MESH,
        )

    def w_copy(k):
        return pltpu.make_async_remote_copy(
            proj, w_buf.at[k], w_send.at[k], w_recv.at[k],
            device_id=(row, lax.rem(col + k, n_col)), device_id_type=MESH,
        )

    def r_copy(h, k):
        target = 2 * row + h
        slot = lax.rem(target - col + n_col, n_col)
        return pltpu.make_async_remote_copy(
            singles.at[pl.ds(h * half, half)], r_buf.at[slot], r_send.at[h, k], r_recv.at[slot],
            device_id=(lax.rem(row + k, n_row), target), device_id_type=MESH,
        )

    def own_copy(h):
        return pltpu.make_async_copy(singles.at[pl.ds(h * half, half)], r_buf.at[0], own_sem)

    def self_case(h):
        return jnp.logical_and(own_right, own_half == h)

    for k in range(1, n_col):
        w_copy(k).start()
        s_copy(k).start()
    for h in (0, 1):
        for k in range(1, n_row):
            r_copy(h, k).start()

        @pl.when(jnp.logical_not(self_case(h)))
        def _():
            r_copy(h, 0).start()

        @pl.when(self_case(h))
        def _():
            own_copy(h).start()

    group = perm.shape[1]
    count = counts[0, col]
    tiles = order.shape[1]
    hit = order[...] == lax.broadcasted_iota(jnp.int32, (tiles, tiles), 0)
    chosen = lax.broadcasted_iota(jnp.int32, (tiles, live_out.shape[1]), 0) < count
    live_out[...] = dot(
        jnp.where(hit, 1.0, 0.0).astype(BF), jnp.where(chosen, 1.0, 0.0).astype(BF)
    )
    place = lax.broadcasted_iota(jnp.int32, (group, group), 0)
    col_hit = jnp.where(perm[pl.ds(col, 1), :] - col * group == place, 1.0, 0.0).astype(BF)
    step_rows = BLOCK_PAIRS // group
    for h in (0, 1):
        index = 2 * row + h
        row_hit = jnp.where(perm[pl.ds(index, 1), :] - index * group == place, 1.0, 0.0).astype(BF)
        part = bins[pl.ds(h * group, group), :].astype(F32).astype(BF)
        wanted = dot(dot_rows(row_hit, part).astype(BF), col_hit)
        for b in range(group // step_rows):
            lanes = [wanted[b * step_rows + i : b * step_rows + i + 1, :] for i in range(step_rows)]
            target_out[h * (group // step_rows) + b] = jnp.concatenate(lanes, axis=1)

    width = proj.shape[1] // 2
    left_sum = dot(singles[...], proj[:, :width])
    for k in range(1, n_col):
        w_copy(k).wait()
        s_copy(k).wait()
        left_sum += dot(s_buf[k], w_buf[k, :, :width])
    left_out[...] = left_sum
    for h in (0, 1):
        for k in range(1, n_row):
            r_copy(h, k).wait_send()

        @pl.when(jnp.logical_not(self_case(h)))
        def _():
            r_copy(h, 0).wait_send()

        @pl.when(self_case(h))
        def _():
            own_copy(h).wait()

    def arrived(k):
        return pltpu.make_async_remote_copy(
            singles.at[pl.ds(0, half)], r_buf.at[k], r_send.at[0, 0], r_recv.at[k],
            device_id=(row, col), device_id_type=MESH,
        )

    @pl.when(jnp.logical_not(own_right))
    def _():
        arrived(0).wait_recv()

    right_sum = dot(r_buf[0], proj[:, width:])
    for k in range(1, n_col):
        arrived(k).wait_recv()
        right_sum += dot(r_buf[k], w_buf[k, :, width:])
    right_out[...] = right_sum.astype(BF).astype(F32)


def run_prologue(n_row, n_col, singles, proj, bins, perm, counts, order):
    rows_dev, chans = singles.shape
    wide = proj.shape[1]
    width = wide // 2
    cols_dev = bins.shape[1]
    tiles = order.shape[1]
    blocks = rows_dev * cols_dev // BLOCK_PAIRS
    dma = pltpu.SemaphoreType.DMA
    return pl.pallas_call(
        functools.partial(prologue, n_row, n_col),
        out_shape=[
            jax.ShapeDtypeStruct((rows_dev, width), F32),
            jax.ShapeDtypeStruct((cols_dev, width), F32),
            jax.ShapeDtypeStruct((blocks, 1, BLOCK_PAIRS), F32),
            jax.ShapeDtypeStruct((tiles, width), F32),
        ],
        in_specs=[VM, VM, VM, VM, SM, VM],
        out_specs=[VM] * 4,
        scratch_shapes=[
            pltpu.VMEM((n_col, rows_dev, chans), BF),
            pltpu.VMEM((n_col, chans, wide), BF),
            pltpu.VMEM((n_col, rows_dev // 2, chans), BF),
            dma((n_col,)), dma((n_col,)), dma((n_col,)), dma((n_col,)),
            dma((2, n_row)), dma((n_col,)), dma,
        ],
        compiler_params=pltpu.CompilerParams(collective_id=0, has_side_effects=True),
        name="prologue",
    )(singles, proj, bins, perm, counts, order)


def layer_norm(field):
    centred = field - jnp.mean(field, axis=-1, keepdims=True)
    scaling = lax.rsqrt(jnp.mean(centred * centred, axis=-1, keepdims=True) + 1e-05)
    return centred * scaling, scaling


def forward(inputs, w_in, w_out, a_ref, d_ref, h_ref):
    hidden = w_out.shape[0]
    total = None
    for c in range(0, hidden, CHUNK):
        here = pl.ds(c, CHUNK)
        gate = dot(inputs, w_in[:, here]).astype(BF)
        up = dot(inputs, w_in[:, pl.ds(hidden + c, CHUNK)]).astype(BF)
        low = gate * BF(0.5)
        twice = jnp.tanh(low) + BF(1)
        act = low * twice
        slope = act + (BF(0.5) * twice) * (BF(1) - act)
        value = act * up
        a_ref[:, here] = act
        d_ref[:, here] = up * slope
        if h_ref is not None:
            h_ref[:, here] = value
        part = dot(value, w_out[here, :])
        total = part if total is None else total + part
    return total


def backward(cot, w_in, w_out, a_ref, d_ref, b_ref):
    hidden = w_out.shape[0]
    total = None
    for c in range(0, hidden, CHUNK):
        here = pl.ds(c, CHUNK)
        there = pl.ds(hidden + c, CHUNK)
        grad_hidden = dot_lanes(cot, w_out[here, :]).astype(BF)
        grad_gate = grad_hidden * d_ref[:, here]
        grad_up = grad_hidden * a_ref[:, here]
        if b_ref is not None:
            b_ref[:, here] = grad_gate
            b_ref[:, there] = grad_up
        part = dot_lanes(grad_gate, w_in[:, here]) + dot_lanes(grad_up, w_in[:, there])
        total = part if total is None else total + part
    return total


def norm_backward(grad, gain, normed, scaling):
    grad = grad * gain
    return scaling * (
        grad
        - jnp.mean(grad, axis=-1, keepdims=True)
        - normed * jnp.mean(grad * normed, axis=-1, keepdims=True)
    )


def grid_step(
    pair, left, right, target, live, g1, w1, w1o, g2, w2, w2o, head,
    pair_grad, left_grad, right_grad, weight_out,
    a1, d1, a2, d2, h2, b2, n1, in_acc, out_acc, head_acc,
):
    pairs, width = pair.shape
    cols = right.shape[0]
    rows = pairs // cols
    step = pl.program_id(0)

    @pl.when(step == 0)
    def _():
        right_grad[...] = jnp.zeros_like(right_grad)
        in_acc[...] = jnp.zeros_like(in_acc)
        out_acc[...] = jnp.zeros_like(out_acc)
        head_acc[...] = jnp.zeros_like(head_acc)

    field = pair[...].astype(F32).reshape(rows, cols, width)
    field = (field + left[...][:, None, :] + right[...][None]).reshape(pairs, width)
    normed, s1 = layer_norm(field)
    n1[...] = normed
    delta = forward((normed * g1[...]).astype(BF), w1, w1o, a1, d1, None)
    second = (field + delta).astype(BF).astype(F32)
    normed2, s2 = layer_norm(second)
    inputs2 = (normed2 * g2[...]).astype(BF)
    delta2 = forward(inputs2, w2, w2o, a2, d2, h2)
    tiles = live.shape[0]
    mask = jnp.broadcast_to(live[...][:, None, :], (tiles, pairs // tiles, width))
    mask = mask.reshape(pairs, width)
    last = (second + mask * delta2).astype(BF)
    logits = dot_lanes(head[...], last)
    exponent = jnp.exp(logits - jnp.max(logits, axis=0, keepdims=True))
    prob = exponent / jnp.sum(exponent, axis=0, keepdims=True)
    bin_id = lax.broadcasted_iota(jnp.int32, logits.shape, 0).astype(F32)
    grad_logits = (prob - jnp.where(target[0] == bin_id, 1.0, 0.0)).astype(BF)
    head_acc[...] += dot(grad_logits, last)
    grad_two = dot_rows(grad_logits, head[...]).astype(BF).astype(F32)
    cot2 = jnp.where(mask > 0, grad_two, 0.0).astype(BF)
    normed_grad = backward(cot2, w2, w2o, a2, d2, b2)
    in_acc[...] += dot_rows(inputs2, b2[...])
    out_acc[...] += dot_rows(cot2, h2[...])
    grad_one = (grad_two + norm_backward(normed_grad, g2[...], normed2, s2)).astype(BF)
    normed_grad = backward(grad_one, w1, w1o, a1, d1, None)
    grad_zero = grad_one.astype(F32) + norm_backward(normed_grad, g1[...], n1[...], s1)
    pair_grad[...] = grad_zero.astype(BF)
    grid = grad_zero.reshape(rows, cols, width)
    right_grad[...] += jnp.sum(grid, axis=0)
    left_grad[...] = jnp.sum(grid, axis=1)

    @pl.when(step == pl.num_programs(0) - 1)
    def _():
        wide = in_acc.shape[1] // width
        for j in range(wide):
            weight_out[j * width : (j + 1) * width, :] = in_acc[:, j * width : (j + 1) * width].astype(BF)
        base = wide * width
        more = out_acc.shape[1] // width
        for j in range(more):
            block = out_acc[:, j * width : (j + 1) * width].T.astype(BF)
            weight_out[base + j * width : base + (j + 1) * width, :] = block
        base = base + more * width
        bins = head_acc.shape[0]
        weight_out[base : base + bins, :] = head_acc[...].astype(BF)
        rest = weight_out.shape[0] - base - bins
        weight_out[base + bins :, :] = jnp.zeros((rest, width), BF)


def run_grid(pay_rows, pair, left, right, target, live, g1, w1, w1o, g2, w2, w2o, head):
    pairs, width = pair.shape
    cols = right.shape[0]
    size = BLOCK_PAIRS
    steps = pairs // size
    rows = size // cols
    tiles = live.shape[0] // steps
    hidden = w1o.shape[0]
    bins = head.shape[0]

    def full(shape):
        return pl.BlockSpec(shape, lambda i: (0,) * len(shape))

    def part(shape):
        return pl.BlockSpec(shape, lambda i: (i,) + (0,) * (len(shape) - 1))

    return pl.pallas_call(
        grid_step,
        grid=(steps,),
        in_specs=[
            part((size, width)), part((rows, width)), full((cols, width)), part((1, 1, size)),
            part((tiles, width)), full((1, width)), full(w1.shape), full(w1o.shape),
            full((1, width)), full(w2.shape), full(w2o.shape), full(head.shape),
        ],
        out_specs=[
            part((size, width)), part((rows, width)), full((cols, width)), full((pay_rows, width)),
        ],
        out_shape=[
            jax.ShapeDtypeStruct((pairs, width), BF),
            jax.ShapeDtypeStruct((pairs // cols, width), F32),
            jax.ShapeDtypeStruct((cols, width), F32),
            jax.ShapeDtypeStruct((pay_rows, width), BF),
        ],
        scratch_shapes=[pltpu.VMEM((size, hidden), BF)] * 5
        + [
            pltpu.VMEM((size, 2 * hidden), BF),
            pltpu.VMEM((size, width), F32),
            pltpu.VMEM((width, 2 * hidden), F32),
            pltpu.VMEM((width, hidden), F32),
            pltpu.VMEM((bins, width), F32),
        ],
        compiler_params=pltpu.CompilerParams(dimension_semantics=("arbitrary",)),
        name="grid",
    )(pair, left, right, target, live, g1, w1, w1o, g2, w2, w2o, head)


def epilogue(
    n_row, n_col,
    weights, left_part, right_part, proj,
    in_out, out_out, head_out, single_out,
    in1, tok1, mid, tok_mid, in2, left2, right_all, left_all, gathered, final,
    send1, recv1, tsend1, trecv1, send2, recv2, lsend2, lrecv2, rsend, rrecv,
    send3, recv3, lsend3, lrecv3, send4, recv4, fsem,
):
    row, col = lax.axis_index("row"), lax.axis_index("col")
    width = weights.shape[1]
    share = weights.shape[0] // n_row
    small = mid.shape[0] // n_col
    tok = tok1.shape[1]
    target_row = col // 2
    self_case = target_row == row
    barrier = pltpu.get_barrier_semaphore()
    for k in range(1, n_row):
        peer = lax.rem(row + k, n_row)
        pl.semaphore_signal(barrier, inc=1, device_id=(peer, col), device_id_type=MESH)
        for h in (0, 1):
            pl.semaphore_signal(barrier, inc=1, device_id=(peer, 2 * row + h), device_id_type=MESH)
    for k in range(1, n_col):
        peer = lax.rem(col + k, n_col)
        pl.semaphore_signal(barrier, inc=1, device_id=(row, peer), device_id_type=MESH)
    for h in (0, 1):

        @pl.when(col != 2 * row + h)
        def _():
            pl.semaphore_signal(barrier, inc=1, device_id=(row, 2 * row + h), device_id_type=MESH)

    pl.semaphore_wait(barrier, n_row + n_col + n_col - 2 - jnp.where(self_case, 1, 0))

    def row_peer(k):
        return lax.rem(row + k, n_row)

    def col_peer(k):
        return lax.rem(col + k, n_col)

    def copy1(k):
        start = pl.multiple_of(row_peer(k) * share, share)
        return pltpu.make_async_remote_copy(
            weights.at[pl.ds(start, share)], in1.at[k], send1.at[k], recv1.at[k],
            device_id=(row_peer(k), col), device_id_type=MESH,
        )

    def tcopy1(k):
        start = pl.multiple_of(row_peer(k) * tok, tok)
        return pltpu.make_async_remote_copy(
            right_part.at[pl.ds(start, tok)], tok1.at[k], tsend1.at[k], trecv1.at[k],
            device_id=(row_peer(k), col), device_id_type=MESH,
        )

    def lcopy2(k):
        start = pl.multiple_of(col_peer(k) * tok, tok)
        return pltpu.make_async_remote_copy(
            left_part.at[pl.ds(start, tok)], left2.at[k], lsend2.at[k], lrecv2.at[k],
            device_id=(row, col_peer(k)), device_id_type=MESH,
        )

    for k in range(1, n_row):
        copy1(k).start()
        tcopy1(k).start()
    for k in range(1, n_col):
        lcopy2(k).start()

    own = right_part[pl.ds(pl.multiple_of(row * tok, tok), tok), :]
    for k in range(1, n_row):
        tcopy1(k).wait()
        own += tok1[k]
    tok_mid[...] = own
    slot = lax.rem(col, 2) * n_row + row

    def rcopy(k):
        return pltpu.make_async_remote_copy(
            tok_mid, right_all.at[slot], rsend.at[k], rrecv.at[slot],
            device_id=(target_row, col_peer(k)), device_id_type=MESH,
        )

    for k in range(1, n_col):
        rcopy(k).start()

    @pl.when(jnp.logical_not(self_case))
    def _():
        rcopy(0).start()

    own = left_part[pl.ds(pl.multiple_of(col * tok, tok), tok), :]
    for k in range(1, n_col):
        lcopy2(k).wait()
        own += left2[k]
    left_all[col] = own

    def lcopy3(k):
        return pltpu.make_async_remote_copy(
            left_all.at[col], left_all.at[col], lsend3.at[k], lrecv3.at[col],
            device_id=(row, col_peer(k)), device_id_type=MESH,
        )

    for k in range(1, n_col):
        lcopy3(k).start()

    total = weights[pl.ds(pl.multiple_of(row * share, share), share), :].astype(F32)
    for k in range(1, n_row):
        copy1(k).wait()
        total += in1[k].astype(F32)
    mid[:share, :] = total.astype(BF)
    mid[share:, :] = jnp.zeros((mid.shape[0] - share, width), BF)

    def copy2(k):
        start = pl.multiple_of(col_peer(k) * small, small)
        return pltpu.make_async_remote_copy(
            mid.at[pl.ds(start, small)], in2.at[k], send2.at[k], recv2.at[k],
            device_id=(row, col_peer(k)), device_id_type=MESH,
        )

    for k in range(1, n_col):
        copy2(k).start()
    total = mid[pl.ds(pl.multiple_of(col * small, small), small), :].astype(F32)
    for k in range(1, n_col):
        copy2(k).wait()
        total += in2[k].astype(F32)
    mine = pl.ds(pl.multiple_of(col * small, small), small)
    gathered[mine, :] = total.astype(BF)

    def copy3(k):
        return pltpu.make_async_remote_copy(
            gathered.at[mine], gathered.at[mine], send3.at[k], recv3.at[col],
            device_id=(row, col_peer(k)), device_id_type=MESH,
        )

    def came3(j):
        spot = pl.ds(pl.multiple_of(j * small, small), small)
        return pltpu.make_async_remote_copy(
            gathered.at[spot], gathered.at[spot], send3.at[0], recv3.at[j],
            device_id=(row, j), device_id_type=MESH,
        )

    for k in range(1, n_col):
        copy3(k).start()
    for k in range(1, n_col):
        came3(col_peer(k)).wait_recv()
    for k in range(1, n_col):
        copy3(k).wait_send()

    band = pl.ds(pl.multiple_of(row * share, share), share)

    def copy4(k):
        return pltpu.make_async_remote_copy(
            gathered.at[pl.ds(0, share)], final.at[band], send4.at[k], recv4.at[row],
            device_id=(row_peer(k), col), device_id_type=MESH,
        )

    def came4(j):
        spot = pl.ds(pl.multiple_of(j * share, share), share)
        return pltpu.make_async_remote_copy(
            gathered.at[pl.ds(0, share)], final.at[spot], send4.at[0], recv4.at[j],
            device_id=(j, col), device_id_type=MESH,
        )

    for k in range(1, n_row):
        copy4(k).start()
    own_copy = pltpu.make_async_copy(gathered.at[pl.ds(0, share)], final.at[band], fsem)
    own_copy.start()

    def lcame(j):
        return pltpu.make_async_remote_copy(
            left_all.at[j], left_all.at[j], lsend3.at[0], lrecv3.at[j],
            device_id=(row, j), device_id_type=MESH,
        )

    def rcame(j):
        return pltpu.make_async_remote_copy(
            tok_mid, right_all.at[j], rsend.at[0], rrecv.at[j],
            device_id=(row, col), device_id_type=MESH,
        )

    for k in range(1, n_col):
        lcame(col_peer(k)).wait_recv()
        lcopy3(k).wait_send()
        rcopy(k).wait_send()

    @pl.when(jnp.logical_not(self_case))
    def _():
        rcopy(0).wait_send()

    for k in range(1, n_col):
        rcame(lax.rem(slot + k, n_col)).wait_recv()

    @pl.when(jnp.logical_not(self_case))
    def _():
        rcame(slot).wait_recv()

    @pl.when(self_case)
    def _():
        right_all[slot] = tok_mid[...]

    tokens = n_col * tok
    left_tok = left_all[...].reshape(tokens, width).astype(BF)
    right_tok = right_all[...].reshape(tokens, width).astype(BF)
    single_out[...] = dot_lanes(left_tok, proj[:, :width]) + dot_lanes(right_tok, proj[:, width:])

    own_copy.wait()
    for k in range(1, n_row):
        came4(row_peer(k)).wait_recv()
    for k in range(1, n_row):
        copy4(k).wait_send()
    scale = 1.0 / (n_row * tokens)
    wide = in_out.shape[1] // width
    for j in range(wide):
        block = final[j * width : (j + 1) * width, :].astype(F32) * scale
        in_out[:, j * width : (j + 1) * width] = block
    base = wide * width
    hidden = out_out.shape[0]
    out_out[...] = final[base : base + hidden, :].astype(F32) * scale
    bins = head_out.shape[0]
    head_out[...] = final[base + hidden : base + hidden + bins, :].astype(F32) * scale


def run_epilogue(n_row, n_col, hidden, bins, weights, left_part, right_part, proj):
    width = weights.shape[1]
    pay = weights.shape[0]
    share = pay // n_row
    rows_dev = left_part.shape[0]
    tok = rows_dev // n_col
    small = -(-share // (16 * n_col)) * 16
    dma = pltpu.SemaphoreType.DMA
    sems = [
        n_row, n_row, n_row, n_row, n_col, n_col, n_col, n_col, n_col, n_col,
        n_col, n_col, n_col, n_col, n_row, n_row,
    ]
    return pl.pallas_call(
        functools.partial(epilogue, n_row, n_col),
        out_shape=[
            jax.ShapeDtypeStruct((width, 2 * hidden), F32),
            jax.ShapeDtypeStruct((hidden, width), F32),
            jax.ShapeDtypeStruct((bins, width), F32),
            jax.ShapeDtypeStruct((rows_dev, proj.shape[0]), F32),
        ],
        in_specs=[VM] * 4,
        out_specs=[VM] * 4,
        scratch_shapes=[
            pltpu.VMEM((n_row, share, width), BF),
            pltpu.VMEM((n_row, tok, width), F32),
            pltpu.VMEM((small * n_col, width), BF),
            pltpu.VMEM((tok, width), F32),
            pltpu.VMEM((n_col, small, width), BF),
            pltpu.VMEM((n_col, tok, width), F32),
            pltpu.VMEM((n_col, tok, width), F32),
            pltpu.VMEM((n_col, tok, width), F32),
            pltpu.VMEM((small * n_col, width), BF),
            pltpu.VMEM((pay, width), BF),
        ]
        + [dma((n,)) for n in sems]
        + [dma],
        compiler_params=pltpu.CompilerParams(collective_id=1, has_side_effects=True),
        name="epilogue",
    )(weights, left_part, right_part, proj)


def local(
    n_row, n_col,
    singles, pair_in, proj_weight, gain_first, first_in, first_out, gain_second, second_in,
    second_out, head_weight, pae_bins, chain_perm, resolved_counts, tile_order,
):
    rows_dev, cols_dev, width = pair_in.shape
    hidden = first_out.shape[0]
    bins = head_weight.shape[1]
    left, right, target, live = run_prologue(
        n_row, n_col, singles, proj_weight, pae_bins, chain_perm.reshape(-1, cols_dev),
        resolved_counts, tile_order,
    )
    need = 3 * hidden + bins
    pay = -(-need // (16 * n_row)) * 16 * n_row
    pair_grad, left_part, right_part, weights = run_grid(
        pay, pair_in.reshape(rows_dev * cols_dev, width), left, right, target, live,
        gain_first.reshape(1, width), first_in, first_out,
        gain_second.reshape(1, width), second_in, second_out, head_weight.T,
    )
    in_grad, out_grad, head_grad, single_grad = run_epilogue(
        n_row, n_col, hidden, bins, weights, left_part, right_part, proj_weight
    )
    return (
        pair_grad.reshape(rows_dev, cols_dev, width), single_grad, in_grad, out_grad, head_grad.T,
    )


def solution(mesh):
    in_specs = (
        P("row", "col"), P("row", "col", None), P("col", None), P(), P(), P(), P(), P(), P(), P(),
        P("row", "col"), P(), P("row", None), P("row", "col"),
    )
    out_specs = (P("row", "col", None), P("row", "col"), P(), P(), P())
    body = functools.partial(local, mesh.shape["row"], mesh.shape["col"])
    return jax.shard_map(body, mesh=mesh, in_specs=in_specs, out_specs=out_specs, check_vma=False)
```

time: 623 us -> 141 us (0.23)
  waiting for transfers between devices: 226 us -> 0 us
  Pallas kernels: 0 us -> 129 us
  matrix products: 115 us -> 0 us
  other arithmetic: 88.6 us -> 0 us
  blocking collectives: 86.7 us -> 0 us
  local copies, waits for them, and re-layouts: 58.9 us -> 10.7 us
  starting transfers between devices: 16.4 us -> 0 us
  between operations: 14.5 us -> 0.66 us
  loops' own time: 12.6 us -> 0 us
    psum x2 -> x0, waiting for transfers between devices: 215 us -> none  [the longest x1 161 us: local(): lax.psum((token_part, weight_sums[0], weight_sums[1], weight_sums[2]), ('...]
    pallas_call x0 -> x3, Pallas kernels: none -> 129 us  [the longest x1 64.3 us: run_grid(): pl.pallas_call(grid_step, grid=(steps,), in_specs=[part((size, width)), p...]
    dot_general x102 -> x0, matrix products: 115 us -> none  [the longest x57 68 us: contract(): lax.dot_general(left_op, right_op, (((left_dim,), (right_dim,)), ((), ())...]
    psum x1 -> x0, blocking collectives: 71.1 us -> none  [local(): lax.psum((token_part, weight_sums[0], weight_sums[1], weight_sums[2]), ('...]
    reduce_sum x70 -> x0, other arithmetic: 48.4 us -> none  [the longest x20 23.1 us: transition_forward(): jnp.mean(centred * centred, axis=-1, keepdims=True) + 1e-05]
    dynamic_slice x45 -> x0, local copies, waits for them, and re-layouts: 22 us -> none  [the longest x16 11.3 us: start_field(): left_rows = lax.dynamic_slice_in_dim(left_part, first_row, block_rows, 0)]
    select_n x12 -> x0, other arithmetic: 18.9 us -> none  [the longest x1 9.98 us: local(): recv_pairs.reshape(col_count * slots, tile_len, width)[flat_index]]
    all_to_all x3 -> x0, starting transfers between devices: 16.1 us -> none  [the longest x1 7.57 us: local(): lax.all_to_all(send_targets, 'col', split_axis=0, concat_axis=0, tiled=True)]
  transfers between devices with their start and end apart: 5 -> 0, of which waited for: 3 -> 0; matrix products, arithmetic and copies ran while one was open for 8% -> 0% of each run, Pallas kernels for 0% -> 0%
where the time goes in v1:
time: 141 us
  Pallas kernels  129 us (91%)
  local copies, waits for them, and re-layouts  10.7 us (8%)
    pallas_call x1, Pallas kernels, run_grid(): pl.pallas_call(grid_step, grid=(steps,), in_specs=[part((size, width)), p...  64.3 us
    pallas_call x1, Pallas kernels, run_epilogue(): pl.pallas_call(functools.partial(epilogue, n_row, n_col), out_shape=[jax....  33.2 us
    pallas_call x1, Pallas kernels, run_prologue(): pl.pallas_call(functools.partial(prologue, n_row, n_col), out_shape=[jax....  31.7 us
    unnamed x6, local copies, waits for them, and re-layouts  9.33 us

profile of v1, /device:TPU:1, one launch (start us, length us, event | category | flops | bytes accessed | tf_op | source)
XLA Modules:
  0.0 140.6 jit_solution(13717915140062205366)
XLA Ops:
  0.6 1.4 reshape.26.perm
  2.0 1.4 %copy.19.singles = bf16[128,24]{1,0:T(8,128)(2,1)} copy(bf16[128,24]{0,1:T(8,128)(2,1)} %param.14) | data formatting | bytes 12288 | tf_op args[0]
  3.4 1.5 %copy.20.bins = s32[128,64]{1,0:T(8,128)} copy(s32[128,64]{0,1:T(8,128)} %param.24) | data formatting | bytes 65536 | tf_op args[10]
  4.9 31.7 %prologue.1 = (f32[128,128]{1,0:T(8,128)}, f32[64,128]{1,0:T(8,128)}, f32[16,1,512]{2,1,0:T(1,128)}, f32[256,128]{1,0:T(8,128)}) custom-call(bf16[128,24]{1,0:T(8,128)(2,1)} %copy.19.singles, bf16[24,256]{1,0:T(8,128)(2,1)} %proj.3, s32[128,64]{1,0:T(8,128)} %copy.20.bins, s32[16,64]{1,0:T(8,128)} %reshape.26.perm, s32[1,16]{1,0:T(1,128)} %counts.1, ...), custom_call_target="tpu_custom_call" | custom-call | tf_op jit(solution)/shard_map/prologue/pallas_call | solution.py:178
  36.6 64.3 %grid.1 = (bf16[8192,128]{1,0:T(8,128)(2,1)}, f32[128,128]{1,0:T(8,128)}, f32[64,128]{1,0:T(8,128)}, bf16[1664,128]{1,0:T(8,128)(2,1)}) custom-call(bf16[8192,128]{1,0:T(8,128)(2,1)} %bitcast.6, f32[128,128]{1,0:T(8,128)} %get-tuple-element.17.left, f32[64,128]{1,0:T(8,128)} %get-tuple-element.18.right, f32[16,1,512]{2,1,0:T(1,128)} %get-tuple-element.19.target, ...), custom_call_target="tpu_custom_call" | custom-call | tf_op jit(solution)/shard_map/grid/pallas_call | solution.py:335
  101.0 33.2 %epilogue.1 = (f32[128,1024]{1,0:T(8,128)}, f32[512,128]{1,0:T(8,128)}, f32[64,128]{1,0:T(8,128)}, f32[128,24]{1,0:T(8,128)}) custom-call(bf16[1664,128]{1,0:T(8,128)(2,1)} %get-tuple-element.22.weights, f32[128,128]{1,0:T(8,128)} %get-tuple-element.23.left_part, f32[64,128]{1,0:T(8,128)} %get-tuple-element.24.right_part, bf16[24,256]{1,0:T(8,128)(2,1)} %proj.3), custom_call_target="tpu_custom_call" | custom-call | tf_op jit(solution)/shard_map/epilogue/pallas_call | solution.py:594
  134.1 1.5 %copy.21 = f32[128,24]{0,1:T(8,128)} copy(f32[128,24]{1,0:T(8,128)} %get-tuple-element.30) | data formatting | bytes 24576
  135.6 1.9 %copy.25 = f32[128,1024]{1,0:T(8,128)} copy(f32[128,1024]{1,0:T(8,128)} %get-tuple-element.41) | data formatting | bytes 1048576
  137.5 1.7 %copy.26 = f32[512,128]{1,0:T(8,128)} copy(f32[512,128]{1,0:T(8,128)} %get-tuple-element.42) | data formatting | bytes 524288
  139.2 1.4 copy.27

commit v2 on v1

--- a/solution.py
+++ b/solution.py
@@ -44,20 +44,22 @@
     s_buf,
     w_buf,
     r_buf,
+    r_full,
     s_send,
     s_recv,
     w_send,
     w_recv,
     r_send,
     r_recv,
-    own_sem,
 ):
     row, col = lax.axis_index("row"), lax.axis_index("col")
-    rows_dev = singles.shape[0]
-    half = rows_dev // 2
+    chans = singles.shape[0]
+    room = s_buf.shape[0] // n_col
     source_row = col // 2
-    own_half = lax.rem(col, 2)
     own_right = source_row == row
+    s_buf[...] = jnp.zeros_like(s_buf)
+    w_buf[...] = jnp.zeros_like(w_buf)
+    r_buf[...] = jnp.zeros_like(r_buf)
     barrier = pltpu.get_barrier_semaphore()
     for k in range(1, n_col):
         peer = lax.rem(col + k, n_col)
@@ -70,31 +72,32 @@
 
     pl.semaphore_wait(barrier, n_col - 1 + 2 * n_row - jnp.where(own_right, 1, 0))
 
+    def spot(k):
+        return pl.ds(k * room, chans)
+
     def s_copy(k):
         return pltpu.make_async_remote_copy(
-            singles, s_buf.at[k], s_send.at[k], s_recv.at[k],
+            singles, s_buf.at[spot(k)], s_send.at[k], s_recv.at[k],
             device_id=(row, lax.rem(col + k, n_col)), device_id_type=MESH,
         )
 
     def w_copy(k):
         return pltpu.make_async_remote_copy(
-            proj, w_buf.at[k], w_send.at[k], w_recv.at[k],
+            proj, w_buf.at[spot(k)], w_send.at[k], w_recv.at[k],
             device_id=(row, lax.rem(col + k, n_col)), device_id_type=MESH,
         )
 
     def r_copy(h, k):
         target = 2 * row + h
         slot = lax.rem(target - col + n_col, n_col)
-        return pltpu.make_async_remote_copy(
-            singles.at[pl.ds(h * half, half)], r_buf.at[slot], r_send.at[h, k], r_recv.at[slot],
+        place = pl.ds(pl.multiple_of(slot * room, room), chans)
+        return pltpu.make_async_remote_copy(
+            singles, r_buf.at[place], r_send.at[h, k], r_recv.at[slot],
             device_id=(lax.rem(row + k, n_row), target), device_id_type=MESH,
         )
 
-    def own_copy(h):
-        return pltpu.make_async_copy(singles.at[pl.ds(h * half, half)], r_buf.at[0], own_sem)
-
-    def self_case(h):
-        return jnp.logical_and(own_right, own_half == h)
+    def other(h):
+        return col != 2 * row + h
 
     for k in range(1, n_col):
         w_copy(k).start()
@@ -103,15 +106,18 @@
         for k in range(1, n_row):
             r_copy(h, k).start()
 
-        @pl.when(jnp.logical_not(self_case(h)))
+        @pl.when(other(h))
         def _():
             r_copy(h, 0).start()
 
-        @pl.when(self_case(h))
-        def _():
-            own_copy(h).start()
-
-    group = perm.shape[1]
+    s_buf[spot(0), :] = singles[...]
+    w_buf[spot(0), :] = proj[...]
+
+    @pl.when(own_right)
+    def _():
+        r_buf[spot(0), :] = singles[...]
+
+    group = bins.shape[0]
     count = counts[0, col]
     tiles = order.shape[1]
     hit = order[...] == lax.broadcasted_iota(jnp.int32, (tiles, tiles), 0)
@@ -120,60 +126,58 @@
         jnp.where(hit, 1.0, 0.0).astype(BF), jnp.where(chosen, 1.0, 0.0).astype(BF)
     )
     place = lax.broadcasted_iota(jnp.int32, (group, group), 0)
-    col_hit = jnp.where(perm[pl.ds(col, 1), :] - col * group == place, 1.0, 0.0).astype(BF)
+    pair_of = perm[pl.ds(source_row, 1), :]
+    mine = jnp.where(lax.rem(col, 2) == 0, pair_of[:, :group], pair_of[:, group:])
+    col_hit = jnp.where(mine - col * group == place, 1.0, 0.0).astype(BF)
+    pair_of = perm[pl.ds(row, 1), :]
     step_rows = BLOCK_PAIRS // group
     for h in (0, 1):
-        index = 2 * row + h
-        row_hit = jnp.where(perm[pl.ds(index, 1), :] - index * group == place, 1.0, 0.0).astype(BF)
-        part = bins[pl.ds(h * group, group), :].astype(F32).astype(BF)
-        wanted = dot(dot_rows(row_hit, part).astype(BF), col_hit)
+        mine = pair_of[:, h * group : (h + 1) * group] - (2 * row + h) * group
+        row_hit = jnp.where(mine == place, 1.0, 0.0).astype(BF)
+        part = bins[:, h * group : (h + 1) * group].astype(F32).astype(BF)
+        wanted = dot_rows(row_hit, dot_rows(part, col_hit).astype(BF))
         for b in range(group // step_rows):
             lanes = [wanted[b * step_rows + i : b * step_rows + i + 1, :] for i in range(step_rows)]
             target_out[h * (group // step_rows) + b] = jnp.concatenate(lanes, axis=1)
 
     width = proj.shape[1] // 2
-    left_sum = dot(singles[...], proj[:, :width])
     for k in range(1, n_col):
         w_copy(k).wait()
         s_copy(k).wait()
-        left_sum += dot(s_buf[k], w_buf[k, :, :width])
-    left_out[...] = left_sum
+    left_out[...] = dot_rows(s_buf[...], w_buf[:, :width])
+
+    def arrived(k):
+        return pltpu.make_async_remote_copy(
+            singles, r_buf.at[spot(k)], r_send.at[0, 0], r_recv.at[k],
+            device_id=(row, col), device_id_type=MESH,
+        )
+
+    @pl.when(jnp.logical_not(own_right))
+    def _():
+        arrived(0).wait_recv()
+
+    for k in range(1, n_col):
+        arrived(k).wait_recv()
+    r_full[...] = dot_rows(r_buf[...], w_buf[:, width:]).astype(BF).astype(F32)
+    half = right_out.shape[0]
+    right_out[...] = r_full[pl.ds(pl.multiple_of(lax.rem(col, 2) * half, half), half), :]
     for h in (0, 1):
         for k in range(1, n_row):
             r_copy(h, k).wait_send()
 
-        @pl.when(jnp.logical_not(self_case(h)))
+        @pl.when(other(h))
         def _():
             r_copy(h, 0).wait_send()
 
-        @pl.when(self_case(h))
-        def _():
-            own_copy(h).wait()
-
-    def arrived(k):
-        return pltpu.make_async_remote_copy(
-            singles.at[pl.ds(0, half)], r_buf.at[k], r_send.at[0, 0], r_recv.at[k],
-            device_id=(row, col), device_id_type=MESH,
-        )
-
-    @pl.when(jnp.logical_not(own_right))
-    def _():
-        arrived(0).wait_recv()
-
-    right_sum = dot(r_buf[0], proj[:, width:])
-    for k in range(1, n_col):
-        arrived(k).wait_recv()
-        right_sum += dot(r_buf[k], w_buf[k, :, width:])
-    right_out[...] = right_sum.astype(BF).astype(F32)
-
 
 def run_prologue(n_row, n_col, singles, proj, bins, perm, counts, order):
-    rows_dev, chans = singles.shape
+    chans, rows_dev = singles.shape
     wide = proj.shape[1]
     width = wide // 2
-    cols_dev = bins.shape[1]
+    cols_dev = bins.shape[0]
     tiles = order.shape[1]
     blocks = rows_dev * cols_dev // BLOCK_PAIRS
+    room = -(-chans // 16) * 16
     dma = pltpu.SemaphoreType.DMA
     return pl.pallas_call(
         functools.partial(prologue, n_row, n_col),
@@ -186,11 +190,12 @@
         in_specs=[VM, VM, VM, VM, SM, VM],
         out_specs=[VM] * 4,
         scratch_shapes=[
-            pltpu.VMEM((n_col, rows_dev, chans), BF),
-            pltpu.VMEM((n_col, chans, wide), BF),
-            pltpu.VMEM((n_col, rows_dev // 2, chans), BF),
+            pltpu.VMEM((n_col * room, rows_dev), BF),
+            pltpu.VMEM((n_col * room, wide), BF),
+            pltpu.VMEM((n_col * room, rows_dev), BF),
+            pltpu.VMEM((rows_dev, width), F32),
             dma((n_col,)), dma((n_col,)), dma((n_col,)), dma((n_col,)),
-            dma((2, n_row)), dma((n_col,)), dma,
+            dma((2, n_row)), dma((n_col,)),
         ],
         compiler_params=pltpu.CompilerParams(collective_id=0, has_side_effects=True),
         name="prologue",
@@ -365,8 +370,8 @@
 def epilogue(
     n_row, n_col,
     weights, left_part, right_part, proj,
-    in_out, out_out, head_out, single_out,
-    in1, tok1, mid, tok_mid, in2, left2, right_all, left_all, gathered, final,
+    final, single_out,
+    in1, tok1, mid, tok_mid, in2, left2, right_all, left_all, gathered,
     send1, recv1, tsend1, trecv1, send2, recv2, lsend2, lrecv2, rsend, rrecv,
     send3, recv3, lsend3, lrecv3, send4, recv4, fsem,
 ):
@@ -560,26 +565,16 @@
     tokens = n_col * tok
     left_tok = left_all[...].reshape(tokens, width).astype(BF)
     right_tok = right_all[...].reshape(tokens, width).astype(BF)
-    single_out[...] = dot_lanes(left_tok, proj[:, :width]) + dot_lanes(right_tok, proj[:, width:])
+    single_out[...] = dot_lanes(proj[:, :width], left_tok) + dot_lanes(proj[:, width:], right_tok)
 
     own_copy.wait()
     for k in range(1, n_row):
         came4(row_peer(k)).wait_recv()
     for k in range(1, n_row):
         copy4(k).wait_send()
-    scale = 1.0 / (n_row * tokens)
-    wide = in_out.shape[1] // width
-    for j in range(wide):
-        block = final[j * width : (j + 1) * width, :].astype(F32) * scale
-        in_out[:, j * width : (j + 1) * width] = block
-    base = wide * width
-    hidden = out_out.shape[0]
-    out_out[...] = final[base : base + hidden, :].astype(F32) * scale
-    bins = head_out.shape[0]
-    head_out[...] = final[base + hidden : base + hidden + bins, :].astype(F32) * scale
-
-
-def run_epilogue(n_row, n_col, hidden, bins, weights, left_part, right_part, proj):
+
+
+def run_epilogue(n_row, n_col, weights, left_part, right_part, proj):
     width = weights.shape[1]
     pay = weights.shape[0]
     share = pay // n_row
@@ -594,13 +589,11 @@
     return pl.pallas_call(
         functools.partial(epilogue, n_row, n_col),
         out_shape=[
-            jax.ShapeDtypeStruct((width, 2 * hidden), F32),
-            jax.ShapeDtypeStruct((hidden, width), F32),
-            jax.ShapeDtypeStruct((bins, width), F32),
-            jax.ShapeDtypeStruct((rows_dev, proj.shape[0]), F32),
+            jax.ShapeDtypeStruct((pay, width), BF),
+            jax.ShapeDtypeStruct((proj.shape[0], rows_dev), F32),
         ],
         in_specs=[VM] * 4,
-        out_specs=[VM] * 4,
+        out_specs=[VM] * 2,
         scratch_shapes=[
             pltpu.VMEM((n_row, share, width), BF),
             pltpu.VMEM((n_row, tok, width), F32),
@@ -611,13 +604,42 @@
             pltpu.VMEM((n_col, tok, width), F32),
             pltpu.VMEM((n_col, tok, width), F32),
             pltpu.VMEM((small * n_col, width), BF),
-            pltpu.VMEM((pay, width), BF),
         ]
         + [dma((n,)) for n in sems]
         + [dma],
         compiler_params=pltpu.CompilerParams(collective_id=1, has_side_effects=True),
         name="epilogue",
     )(weights, left_part, right_part, proj)
+
+
+def finish(scale, sums, single, in_out, out_out, head_out, single_out):
+    width = sums.shape[1]
+    wide = in_out.shape[1] // width
+    for j in range(wide):
+        block = sums[j * width : (j + 1) * width, :].astype(F32) * scale
+        in_out[:, j * width : (j + 1) * width] = block
+    base = wide * width
+    hidden = out_out.shape[0]
+    out_out[...] = sums[base : base + hidden, :].astype(F32) * scale
+    bins = head_out.shape[0]
+    head_out[...] = sums[base + hidden : base + hidden + bins, :].astype(F32) * scale
+    single_out[...] = single[...]
+
+
+def run_finish(tokens, hidden, bins, sums, single):
+    width = sums.shape[1]
+    return pl.pallas_call(
+        functools.partial(finish, 1.0 / tokens),
+        out_shape=[
+            jax.ShapeDtypeStruct((width, 2 * hidden), F32),
+            jax.ShapeDtypeStruct((hidden, width), F32),
+            jax.ShapeDtypeStruct((bins, width), F32),
+            jax.ShapeDtypeStruct(single.shape, F32),
+        ],
+        in_specs=[VM] * 2,
+        out_specs=[VM] * 4,
+        name="finish",
+    )(sums, single)
 
 
 def local(
@@ -629,7 +651,7 @@
     hidden = first_out.shape[0]
     bins = head_weight.shape[1]
     left, right, target, live = run_prologue(
-        n_row, n_col, singles, proj_weight, pae_bins, chain_perm.reshape(-1, cols_dev),
+        n_row, n_col, singles.T, proj_weight, pae_bins.T, chain_perm.reshape(n_row, -1),
         resolved_counts, tile_order,
     )
     need = 3 * hidden + bins
@@ -639,11 +661,12 @@
         gain_first.reshape(1, width), first_in, first_out,
         gain_second.reshape(1, width), second_in, second_out, head_weight.T,
     )
-    in_grad, out_grad, head_grad, single_grad = run_epilogue(
-        n_row, n_col, hidden, bins, weights, left_part, right_part, proj_weight
+    sums, single = run_epilogue(n_row, n_col, weights, left_part, right_part, proj_weight)
+    in_grad, out_grad, head_grad, single_grad = run_finish(
+        chain_perm.shape[0], hidden, bins, sums, single
     )
     return (
-        pair_grad.reshape(rows_dev, cols_dev, width), single_grad, in_grad, out_grad, head_grad.T,
+        pair_grad.reshape(rows_dev, cols_dev, width), single_grad.T, in_grad, out_grad, head_grad.T,
     )
 
 

time: 141 us -> 121 us (0.86)
  local copies, waits for them, and re-layouts: 10.7 us -> 0 us
  Pallas kernels: 129 us -> 120 us
    pallas_call x1, Pallas kernels: 31.7 us -> 20.5 us  [run_prologue(): pl.pallas_call(functools.partial(prologue, n_row, n_col), out_shape=[jax....]
    unnamed x6 -> x0, local copies, waits for them, and re-layouts: 9.33 us -> none
    pallas_call x0 -> x1, Pallas kernels: none -> 1.92 us  [run_finish(): pl.pallas_call(functools.partial(finish, 1.0 / tokens), out_shape=[jax.Sh...]
where the time goes in v2:
time: 121 us
  Pallas kernels  120 us (99%)
    pallas_call x1, Pallas kernels, run_grid(): pl.pallas_call(grid_step, grid=(steps,), in_specs=[part((size, width)), p...  64.3 us
    pallas_call x1, Pallas kernels, run_epilogue(): pl.pallas_call(functools.partial(epilogue, n_row, n_col), out_shape=[jax....  33.6 us
    pallas_call x1, Pallas kernels, run_prologue(): pl.pallas_call(functools.partial(prologue, n_row, n_col), out_shape=[jax....  20.5 us

profile of v2, /device:TPU:1, one launch (start us, length us, event | category | flops | bytes accessed | tf_op | source)
XLA Modules:
  0.0 121.0 jit_solution(5971577105996448603)
XLA Ops:
  0.6 20.5 %prologue.1 = (f32[128,128]{1,0:T(8,128)}, f32[64,128]{1,0:T(8,128)}, f32[16,1,512]{2,1,0:T(1,128)}, f32[256,128]{1,0:T(8,128)}) custom-call(bf16[24,128]{1,0:T(8,128)(2,1)} %bitcast.13, bf16[24,256]{1,0:T(8,128)(2,1)} %proj.3, s32[64,128]{1,0:T(8,128)} %bitcast.11, s32[8,128]{1,0:T(8,128)} %bitcast.14, s32[1,16]{1,0:T(1,128)} %counts.1, s32[1,256]{1,0:T(1,128)} %order.1), custom_call_target="tpu_custom_call" | custom-call | tf_op jit(solution)/shard_map/prologue/pallas_call | solution.py:182
  21.1 64.3 %grid.1 = (bf16[8192,128]{1,0:T(8,128)(2,1)}, f32[128,128]{1,0:T(8,128)}, f32[64,128]{1,0:T(8,128)}, bf16[1664,128]{1,0:T(8,128)(2,1)}) custom-call(bf16[8192,128]{1,0:T(8,128)(2,1)} %bitcast.10, f32[128,128]{1,0:T(8,128)} %get-tuple-element.19.left, f32[64,128]{1,0:T(8,128)} %get-tuple-element.20.right, f32[16,1,512]{2,1,0:T(1,128)} %get-tuple-element.21.target, ...), custom_call_target="tpu_custom_call" | custom-call | tf_op jit(solution)/shard_map/grid/pallas_call | solution.py:340
  85.5 33.6 %epilogue.1 = (bf16[1664,128]{1,0:T(8,128)(2,1)}, f32[24,128]{1,0:T(8,128)}) custom-call(bf16[1664,128]{1,0:T(8,128)(2,1)} %get-tuple-element.24.weights, f32[128,128]{1,0:T(8,128)} %get-tuple-element.25.left_part, f32[64,128]{1,0:T(8,128)} %get-tuple-element.26.right_part, bf16[24,256]{1,0:T(8,128)(2,1)} %proj.3), custom_call_target="tpu_custom_call" | custom-call | tf_op jit(solution)/shard_map/epilogue/pallas_call | solution.py:589
  119.1 1.9 %finish.1 = (f32[128,1024]{1,0:T(8,128)}, f32[512,128]{1,0:T(8,128)}, f32[64,128]{1,0:T(8,128)}, f32[24,128]{1,0:T(8,128)}) custom-call(bf16[1664,128]{1,0:T(8,128)(2,1)} %get-tuple-element.27.sums, f32[24,128]{1,0:T(8,128)} %get-tuple-element.28.single), custom_call_target="tpu_custom_call" | custom-call | tf_op jit(solution)/shard_map/finish/pallas_call | solution.py:631

commit v3 on v2

--- a/solution.py
+++ b/solution.py
@@ -8,6 +8,7 @@
 
 TILE = 32
 BLOCK_PAIRS = 512
+STREAMS = 4
 CHUNK = 256
 MESH = pl.DeviceIdType.MESH
 BF = jnp.bfloat16
@@ -255,54 +256,88 @@
     )
 
 
-def grid_step(
-    pair, left, right, target, live, g1, w1, w1o, g2, w2, w2o, head,
-    pair_grad, left_grad, right_grad, weight_out,
-    a1, d1, a2, d2, h2, b2, n1, in_acc, out_acc, head_acc,
+def stream(
+    here, pair, left, right, target, live, g1, w1, w1o, g2, w2, w2o, head,
+    pair_grad, left_grad, right_grad, in_acc, out_acc, head_acc,
+    a1, d1, a2, d2, h2, b2, n1,
 ):
-    pairs, width = pair.shape
+    rows_here, tiles_here = here[1], here[2]
+    width = pair.shape[1]
     cols = right.shape[0]
+    pairs = here[0].size
     rows = pairs // cols
-    step = pl.program_id(0)
-
-    @pl.when(step == 0)
-    def _():
-        right_grad[...] = jnp.zeros_like(right_grad)
-        in_acc[...] = jnp.zeros_like(in_acc)
-        out_acc[...] = jnp.zeros_like(out_acc)
-        head_acc[...] = jnp.zeros_like(head_acc)
-
-    field = pair[...].astype(F32).reshape(rows, cols, width)
-    field = (field + left[...][:, None, :] + right[...][None]).reshape(pairs, width)
+    field = pair[here[0], :].astype(F32).reshape(rows, cols, width)
+    field = (field + left[rows_here, :][:, None, :] + right[...][None]).reshape(pairs, width)
     normed, s1 = layer_norm(field)
     n1[...] = normed
-    delta = forward((normed * g1[...]).astype(BF), w1, w1o, a1, d1, None)
+    inputs1 = (normed * g1[...]).astype(BF)
+    yield
+    delta = forward(inputs1, w1, w1o, a1, d1, None)
+    yield
     second = (field + delta).astype(BF).astype(F32)
     normed2, s2 = layer_norm(second)
     inputs2 = (normed2 * g2[...]).astype(BF)
+    yield
     delta2 = forward(inputs2, w2, w2o, a2, d2, h2)
-    tiles = live.shape[0]
-    mask = jnp.broadcast_to(live[...][:, None, :], (tiles, pairs // tiles, width))
+    yield
+    tiles = tiles_here.size
+    mask = jnp.broadcast_to(live[tiles_here, :][:, None, :], (tiles, pairs // tiles, width))
     mask = mask.reshape(pairs, width)
     last = (second + mask * delta2).astype(BF)
     logits = dot_lanes(head[...], last)
     exponent = jnp.exp(logits - jnp.max(logits, axis=0, keepdims=True))
     prob = exponent / jnp.sum(exponent, axis=0, keepdims=True)
     bin_id = lax.broadcasted_iota(jnp.int32, logits.shape, 0).astype(F32)
-    grad_logits = (prob - jnp.where(target[0] == bin_id, 1.0, 0.0)).astype(BF)
+    grad_logits = (prob - jnp.where(target[here[3]] == bin_id, 1.0, 0.0)).astype(BF)
     head_acc[...] += dot(grad_logits, last)
     grad_two = dot_rows(grad_logits, head[...]).astype(BF).astype(F32)
     cot2 = jnp.where(mask > 0, grad_two, 0.0).astype(BF)
+    yield
     normed_grad = backward(cot2, w2, w2o, a2, d2, b2)
+    yield
     in_acc[...] += dot_rows(inputs2, b2[...])
     out_acc[...] += dot_rows(cot2, h2[...])
     grad_one = (grad_two + norm_backward(normed_grad, g2[...], normed2, s2)).astype(BF)
+    yield
     normed_grad = backward(grad_one, w1, w1o, a1, d1, None)
+    yield
     grad_zero = grad_one.astype(F32) + norm_backward(normed_grad, g1[...], n1[...], s1)
-    pair_grad[...] = grad_zero.astype(BF)
+    pair_grad[here[0], :] = grad_zero.astype(BF)
     grid = grad_zero.reshape(rows, cols, width)
     right_grad[...] += jnp.sum(grid, axis=0)
-    left_grad[...] = jnp.sum(grid, axis=1)
+    left_grad[rows_here, :] = jnp.sum(grid, axis=1)
+    yield
+
+
+def grid_step(
+    pair, left, right, target, live, g1, w1, w1o, g2, w2, w2o, head,
+    pair_grad, left_grad, right_grad, weight_out, in_acc, out_acc, head_acc, *scratch,
+):
+    width = pair.shape[1]
+    step = pl.program_id(0)
+
+    @pl.when(step == 0)
+    def _():
+        right_grad[...] = jnp.zeros_like(right_grad)
+        in_acc[...] = jnp.zeros_like(in_acc)
+        out_acc[...] = jnp.zeros_like(out_acc)
+        head_acc[...] = jnp.zeros_like(head_acc)
+
+    each = len(scratch) // STREAMS
+    pairs, rows = BLOCK_PAIRS, left.shape[0] // STREAMS
+    tiles = live.shape[0] // STREAMS
+    streams = []
+    for k in range(STREAMS):
+        here = (pl.ds(k * pairs, pairs), pl.ds(k * rows, rows), pl.ds(k * tiles, tiles), k)
+        streams.append(
+            stream(
+                here, pair, left, right, target, live, g1, w1, w1o, g2, w2, w2o, head,
+                pair_grad, left_grad, right_grad, in_acc, out_acc, head_acc,
+                *scratch[k * each : (k + 1) * each],
+            )
+        )
+    for _ in zip(*streams):
+        pass
 
     @pl.when(step == pl.num_programs(0) - 1)
     def _():
@@ -324,7 +359,7 @@
 def run_grid(pay_rows, pair, left, right, target, live, g1, w1, w1o, g2, w2, w2o, head):
     pairs, width = pair.shape
     cols = right.shape[0]
-    size = BLOCK_PAIRS
+    size = BLOCK_PAIRS * STREAMS
     steps = pairs // size
     rows = size // cols
     tiles = live.shape[0] // steps
@@ -341,7 +376,7 @@
         grid_step,
         grid=(steps,),
         in_specs=[
-            part((size, width)), part((rows, width)), full((cols, width)), part((1, 1, size)),
+            part((size, width)), part((rows, width)), full((cols, width)), part((STREAMS, 1, BLOCK_PAIRS)),
             part((tiles, width)), full((1, width)), full(w1.shape), full(w1o.shape),
             full((1, width)), full(w2.shape), full(w2o.shape), full(head.shape),
         ],
@@ -354,14 +389,16 @@
             jax.ShapeDtypeStruct((cols, width), F32),
             jax.ShapeDtypeStruct((pay_rows, width), BF),
         ],
-        scratch_shapes=[pltpu.VMEM((size, hidden), BF)] * 5
-        + [
-            pltpu.VMEM((size, 2 * hidden), BF),
-            pltpu.VMEM((size, width), F32),
+        scratch_shapes=[
             pltpu.VMEM((width, 2 * hidden), F32),
             pltpu.VMEM((width, hidden), F32),
             pltpu.VMEM((bins, width), F32),
-        ],
+        ]
+        + (
+            [pltpu.VMEM((BLOCK_PAIRS, hidden), BF)] * 5
+            + [pltpu.VMEM((BLOCK_PAIRS, 2 * hidden), BF), pltpu.VMEM((BLOCK_PAIRS, width), F32)]
+        )
+        * STREAMS,
         compiler_params=pltpu.CompilerParams(dimension_semantics=("arbitrary",)),
         name="grid",
     )(pair, left, right, target, live, g1, w1, w1o, g2, w2, w2o, head)

time: 121 us -> 96.6 us (0.80)
  Pallas kernels: 120 us -> 95.7 us
    pallas_call x1, Pallas kernels: 64.3 us -> 39.7 us  [run_grid(): pl.pallas_call(grid_step, grid=(steps,), in_specs=[part((size, width)), p...]
where the time goes in v3:
time: 96.6 us; the launch traced here: 96.4 us
  Pallas kernels  95.7 us (99%)
    pallas_call x1, Pallas kernels, run_grid(): pl.pallas_call(grid_step, grid=(steps,), in_specs=[part((size, width)), p...  39.7 us
    pallas_call x1, Pallas kernels, run_epilogue(): pl.pallas_call(functools.partial(epilogue, n_row, n_col), out_shape=[jax....  33.6 us
    pallas_call x1, Pallas kernels, run_prologue(): pl.pallas_call(functools.partial(prologue, n_row, n_col), out_shape=[jax....  20.5 us

profile of v3, /device:TPU:1, one launch (start us, length us, event | category | flops | bytes accessed | tf_op | source)
XLA Modules:
  0.0 96.4 jit_solution(14436431329311800746)
XLA Ops:
  0.6 20.5 %prologue.1 = (f32[128,128]{1,0:T(8,128)}, f32[64,128]{1,0:T(8,128)}, f32[16,1,512]{2,1,0:T(1,128)}, f32[256,128]{1,0:T(8,128)}) custom-call(bf16[24,128]{1,0:T(8,128)(2,1)} %bitcast.13, bf16[24,256]{1,0:T(8,128)(2,1)} %proj.3, s32[64,128]{1,0:T(8,128)} %bitcast.11, s32[8,128]{1,0:T(8,128)} %bitcast.14, s32[1,16]{1,0:T(1,128)} %counts.1, s32[1,256]{1,0:T(1,128)} %order.1), custom_call_target="tpu_custom_call" | custom-call | tf_op jit(solution)/shard_map/prologue/pallas_call | solution.py:183
  21.1 39.7 %grid.1 = (bf16[8192,128]{1,0:T(8,128)(2,1)}, f32[128,128]{1,0:T(8,128)}, f32[64,128]{1,0:T(8,128)}, bf16[1664,128]{1,0:T(8,128)(2,1)}) custom-call(bf16[8192,128]{1,0:T(8,128)(2,1)} %bitcast.10, f32[128,128]{1,0:T(8,128)} %get-tuple-element.19.left, f32[64,128]{1,0:T(8,128)} %get-tuple-element.20.right, f32[16,1,512]{2,1,0:T(1,128)} %get-tuple-element.21.target, ...), custom_call_target="tpu_custom_call" | custom-call | tf_op jit(solution)/shard_map/grid/pallas_call | solution.py:375
  60.8 33.6 %epilogue.1 = (bf16[1664,128]{1,0:T(8,128)(2,1)}, f32[24,128]{1,0:T(8,128)}) custom-call(bf16[1664,128]{1,0:T(8,128)(2,1)} %get-tuple-element.24.weights, f32[128,128]{1,0:T(8,128)} %get-tuple-element.25.left_part, f32[64,128]{1,0:T(8,128)} %get-tuple-element.26.right_part, bf16[24,256]{1,0:T(8,128)(2,1)} %proj.3), custom_call_target="tpu_custom_call" | custom-call | tf_op jit(solution)/shard_map/epilogue/pallas_call | solution.py:626
  94.5 1.9 %finish.1 = (f32[128,1024]{1,0:T(8,128)}, f32[512,128]{1,0:T(8,128)}, f32[64,128]{1,0:T(8,128)}, f32[24,128]{1,0:T(8,128)}) custom-call(bf16[1664,128]{1,0:T(8,128)(2,1)} %get-tuple-element.27.sums, f32[24,128]{1,0:T(8,128)} %get-tuple-element.28.single), custom_call_target="tpu_custom_call" | custom-call | tf_op jit(solution)/shard_map/finish/pallas_call | solution.py:668
